TPU v7x, 32 devices: a whole 2x2x4 slice. The times are simulated.
32 devices in a mesh: island: 8 (over z, x), fsdp: 4 (over y, core).
Axes of the slice: x: 2, y: 2, z: 4, core: 2. Of those that a mesh axis runs over, the one named last changes fastest.
Arguments:
- local_weights: bfloat16 [8, 4096, 512], P('island', 'fsdp'), may hold values from -6 to 6
- adam_first: bfloat16 [8, 4096, 512], P('island', 'fsdp'), may hold values from -6 to 6
- adam_second: bfloat16 [8, 4096, 512], P('island', 'fsdp'), may hold values from 0.5 to 4
- global_weights: float32 [4096, 512], P('fsdp'), may hold values from -6 to 6
- outer_momentum: float32 [4096, 512], P('fsdp'), may hold values from -3 to 3
- inputs: bfloat16 [8, 512, 4096], P('island', 'fsdp'), may hold values from -6 to 6
- key_cotangent: bfloat16 [8, 512, 512], P('island', 'fsdp'), may hold values from -24 to 24
Outputs:
- new_local: bfloat16 [8, 4096, 512], P('island', 'fsdp')
- new_first: bfloat16 [8, 4096, 512], P('island', 'fsdp')
- new_second: bfloat16 [8, 4096, 512], P('island', 'fsdp')
- new_global: float32 [4096, 512], P('fsdp')
- new_momentum: float32 [4096, 512], P('fsdp')
All inputs are finite; a program needn't handle non-finite values.
Results may differ from a plain program's by a relative error of at most 0.0065.
Values may be sent and summed in bfloat16 or wider, within the bound.
A program may use at most 64 MiB of HBM per device.

v0:
```python
import jax
import jax.numpy as jnp
from jax import lax
from jax.sharding import PartitionSpec as P

HEAD_DIM = 128
beta_one = 0.9
beta_two = 0.95
inner_rate = 0.02
weight_decay = 0.1
adam_epsilon = 1e-08
norm_epsilon = 1e-06
outer_rate = 0.7
outer_beta = 0.9
merge_weight = 0.5


def key_backward(keys, upstream):
    heads = keys.shape[1] // HEAD_DIM
    shaped = keys.reshape(keys.shape[0], heads, HEAD_DIM)
    cotan_heads = upstream.reshape(keys.shape[0], heads, HEAD_DIM)
    squares = jnp.mean(shaped * shaped, axis=-1, keepdims=True)
    inverse = lax.rsqrt(squares + norm_epsilon)
    normed = shaped * inverse
    projected = jnp.mean(cotan_heads * normed, axis=-1, keepdims=True)
    return (inverse * (cotan_heads - normed * projected)).reshape(keys.shape)


def local(
    local_weights, adam_first, adam_second, global_weights, outer_momentum, inputs, key_cotangent
):
    weights = local_weights[0]
    tokens = inputs[0]
    upstream = key_cotangent[0].astype(jnp.float32)
    scale = float(tokens.shape[1]) ** (-0.5)
    islands = lax.axis_size("island")
    summed = lax.psum(weights.astype(jnp.float32), "island")
    outer_grad = global_weights - summed / islands
    new_momentum = outer_beta * outer_momentum + outer_grad
    new_global = global_weights - outer_rate * (outer_grad + outer_beta * new_momentum)
    columns = tokens
    keys = (
        jnp.dot(
            columns,
            lax.all_gather(weights, "fsdp", axis=0, tiled=True),
            preferred_element_type=jnp.float32,
        )
        * scale
    )
    key_grad = (key_backward(keys, upstream) * scale).astype(jnp.bfloat16)
    columns = tokens
    gradient = lax.psum_scatter(
        lax.dot_general(
            columns, key_grad, (((0,), (0,)), ((), ())), preferred_element_type=jnp.float32
        ).astype(jnp.bfloat16),
        "fsdp",
        scatter_dimension=0,
        tiled=True,
    ).astype(jnp.float32)
    first_new = beta_one * adam_first[0].astype(jnp.float32) + (1.0 - beta_one) * gradient
    second_new = (
        beta_two * adam_second[0].astype(jnp.float32) + (1.0 - beta_two) * gradient * gradient
    )
    current = weights.astype(jnp.float32)
    inner = current - inner_rate * (
        first_new / (jnp.sqrt(second_new) + adam_epsilon) + weight_decay * current
    )
    merged = merge_weight * inner + (1.0 - merge_weight) * new_global
    return (
        merged.astype(jnp.bfloat16)[None],
        first_new.astype(jnp.bfloat16)[None],
        second_new.astype(jnp.bfloat16)[None],
        new_global,
        new_momentum,
    )


def solution(mesh):
    placed = (
        P("island", "fsdp", None),
        P("island", "fsdp", None),
        P("island", "fsdp", None),
        P("fsdp", None),
        P("fsdp", None),
        P("island", "fsdp", None),
        P("island", "fsdp", None),
    )
    return jax.shard_map(
        local,
        mesh=mesh,
        in_specs=placed,
        out_specs=(
            P("island", "fsdp", None),
            P("island", "fsdp", None),
            P("island", "fsdp", None),
            P("fsdp", None),
            P("fsdp", None),
        ),
        check_vma=False,
    )
```

profile of v0, /device:TPU:0, one launch (start us, length us, event | category | flops | bytes accessed | tf_op | source)
XLA Modules:
  0.0 142.2 jit_solution(9254017359627056663)
XLA Ops:
  8.0 0.0 copy-start
  8.0 0.0 all-gather.3.cloned.1.call-start
  8.1 0.7 all-gather.3.cloned.1.call-update
  8.7 0.0 all-reduce.2.cloned.1.call-start
  8.8 1.5 %copy.12 = bf16[1,1024,512]{1,2,0:T(8,128)(2,1)S(1)} copy(bf16[1,1024,512]{2,1,0:T(8,128)(2,1)} %param.7) | data formatting | bytes 2097152 | tf_op args[0]
  10.3 0.0 copy-start.3
  10.3 1.6 %bitcast_convert_fusion = f32[1024,512]{0,1:T(8,128)} fusion(bf16[1,1024,512]{1,2,0:T(8,128)(2,1)S(1)} %copy.12), kind=kLoop, calls=%fused_computation.17 | loop fusion | flops 524288 | bytes 3145728 | tf_op jit(solution)/shard_map/convert_element_type | solution.py:64
  11.9 0.0 all-reduce.2.cloned.1.call-update
  11.9 0.0 reduce-scatter.2.cloned.1.call-start
  12.0 0.1 reshape.52
  12.1 35.5 %all-gather.3.cloned.1.call-done = bf16[1,4096,512]{2,1,0:T(8,128)(2,1)} async-done(((bf16[1,1024,512]{2,1,0:T(8,128)(2,1)}), bf16[1,4096,512]{2,1,0:T(8,128)(2,1)}) %all-gather.3.cloned.1.call-update) | async-done | bytes 4194320 | tf_op jit(solution)/shard_map/all_gather | solution.py:45
  47.6 0.0 copy-done
  47.6 2.9 %fusion.7 = f32[128,512]{1,0:T(8,128)S(1)} fusion(bf16[1,4096,512]{2,1,0:T(8,128)(2,1)} %all-gather.3.cloned.1.call-done, bf16[1,128,4096]{2,1,0:T(8,128)(2,1)S(1)} %copy-done), kind=kOutput, calls=%fused_computation.14 | convolution fusion | flops 536936448 | bytes 5505024 | tf_op jit(solution)/shard_map/dot_general | solution.py:43
  50.5 0.1 reshape.50
  50.6 0.2 multiply_reduce_fusion.1
  50.8 0.4 multiply_reduce_fusion
  51.2 0.2 mul.112
  51.4 0.2 mul.107
  51.6 3.3 %fusion = bf16[4096,512]{0,1:T(8,128)(2,1)} fusion(bf16[1,128,4096]{2,1,0:T(8,128)(2,1)S(1)} %copy-done, f32[16,8,4,128]{3,2,1,0:T(4,128)S(1)} %bitcast.65, f32[128,512]{1,0:T(8,128)S(1)} %fusion.7, f32[16,8,4,128]{3,2,1,0:T(4,128)S(1)} %bitcast.66, bf16[1,128,512]{2,1,0:T(8,128)(2,1)S(1)} %copy-done.3), kind=kOutput, calls=%fused_computation.1 | convolution fusion | flops 539426816 | bytes 6160384 | tf_op jit(solution)/shard_map/dot_general | solution.py:53
  54.9 0.0 reduce-scatter.2.cloned.1.call-update
  54.9 2.9 %copy.16 = f32[1024,512]{0,1:T(8,128)} copy(f32[1024,512]{1,0:T(8,128)} %param.11) | data formatting | bytes 4194304 | tf_op args[4]
  57.8 2.9 %copy.17 = f32[1024,512]{0,1:T(8,128)} copy(f32[1024,512]{1,0:T(8,128)} %param.10) | data formatting | bytes 4194304 | tf_op args[3]
  60.7 1.5 %copy.13 = bf16[1,1024,512]{1,2,0:T(8,128)(2,1)S(1)} copy(bf16[1,1024,512]{2,1,0:T(8,128)(2,1)} %param.8) | data formatting | bytes 2097152 | tf_op args[1]
  62.3 2.5 %copy.14 = bf16[1,1024,512]{1,2,0:T(8,128)(2,1)} copy(bf16[1,1024,512]{2,1,0:T(8,128)(2,1)} %param.9) | data formatting | bytes 2097152 | tf_op args[2]
  64.8 52.7 %all-reduce.2.cloned.1.call-done = f32[1024,512]{0,1:T(8,128)} async-done(((f32[1024,512]{0,1:T(8,128)}), f32[1024,512]{0,1:T(8,128)}) %all-reduce.2.cloned.1.call-update) | async-done | bytes 2097168 | tf_op jit(solution)/shard_map/psum | solution.py:37
  117.5 6.4 %fusion.14 = (bf16[1,1024,512]{1,2,0:T(8,128)(2,1)}, f32[1024,512]{0,1:T(8,128)}, f32[1024,512]{0,1:T(8,128)}, bf16[1,1024,512]{1,2,0:T(8,128)(2,1)}, bf16[1,1024,512]{1,2,0:T(8,128)(2,1)}) fusion(bf16[1,1024,512]{1,2,0:T(8,128)(2,1)} %copy.14, bf16[1024,512]{0,1:T(8,128)(2,1)} %reduce-scatter.2.cloned.1.call-done, bf16[1,1024,512]{1,2,0:T(8,128)(2,1)S(1)} %copy.13, ...), kind=kLoop, calls=%fused_computation.20 | loop fusion | flops 15728640 | bytes 17825792 | tf_op jit(solution)/shard_map/broadcast_in_dim | solution.py:70
  123.9 2.9 %copy.21 = f32[1024,512]{1,0:T(8,128)} copy(f32[1024,512]{0,1:T(8,128)} %get-tuple-element.11) | data formatting | bytes 4194304
  126.8 2.9 %copy.22 = f32[1024,512]{1,0:T(8,128)} copy(f32[1024,512]{0,1:T(8,128)} %get-tuple-element.12) | data formatting | bytes 4194304
  129.7 2.4 %copy.18 = bf16[1,1024,512]{2,1,0:T(8,128)(2,1)} copy(bf16[1,1024,512]{1,2,0:T(8,128)(2,1)} %get-tuple-element.10) | data formatting | bytes 2097152
  132.1 1.3 copy.19
  133.4 0.0 copy-done.1
  133.4 1.3 copy.20
  (7 shorter events, 0.0 us)
Async XLA Ops:
  8.0 39.6 %copy-start = (bf16[1,128,4096]{2,1,0:T(8,128)(2,1)S(1)}, bf16[1,128,4096]{2,1,0:T(8,128)(2,1)}, u32[]{:S(2)}) copy-start(bf16[1,128,4096]{2,1,0:T(8,128)(2,1)} %param.12) | copy-start | bytes 3145732
  8.0 39.6 %all-gather.3.cloned.1.call-start = ((), (), s32[]{:S(2)}) async-start(), calls=%async_computation.3 | async-start | bytes 5242880 | tf_op jit(solution)/shard_map/all_gather | solution.py:45
  8.7 108.8 %all-reduce.2.cloned.1.call-start = ((), (), s32[]{:S(2)}) async-start(), calls=%async_computation.2 | async-start | bytes 4194304 | tf_op jit(solution)/shard_map/psum | solution.py:37
  10.3 1.7 %copy-start.3 = (bf16[1,128,512]{2,1,0:T(8,128)(2,1)S(1)}, bf16[1,128,512]{2,1,0:T(8,128)(2,1)}, u32[]{:S(2)}) copy-start(bf16[1,128,512]{2,1,0:T(8,128)(2,1)} %param.13) | copy-start | bytes 393220
  11.9 105.6 %reduce-scatter.2.cloned.1.call-start = ((), (), s32[]{:S(2)}) async-start(), calls=%async_computation.1 | async-start | bytes 5242880 | tf_op jit(solution)/shard_map/reduce_scatter | solution.py:52
  129.7 2.4 %copy-start.2 = (bf16[1,1024,512]{1,2,0:T(8,128)(2,1)S(1)}, bf16[1,1024,512]{1,2,0:T(8,128)(2,1)}, u32[]{:S(2)}) copy-start(bf16[1,1024,512]{1,2,0:T(8,128)(2,1)} %get-tuple-element.14) | copy-start | bytes 3145732
  129.7 3.7 %copy-start.1 = (bf16[1,1024,512]{1,2,0:T(8,128)(2,1)S(1)}, bf16[1,1024,512]{1,2,0:T(8,128)(2,1)}, u32[]{:S(2)}) copy-start(bf16[1,1024,512]{1,2,0:T(8,128)(2,1)} %get-tuple-element.13) | copy-start | bytes 3145732
Sparse Core Ops, SparseCore 0:
  10.4 37.1 all-gather.2
  55.0 44.4 reduce-scatter.1
Sparse Core Ops, SparseCore 1:
  12.8 104.6 all-reduce.1
where the time goes:
time: 143 us; the launch traced here: 142 us
  waiting for transfers between devices  88.9 us (62%)
  local copies, waits for them, and re-layouts  22.8 us (16%)
  between operations  15.6 us (11%)
  other arithmetic  8.62 us (6%)
  matrix products  6.16 us (4%)
    psum x1, waiting for transfers between devices, local(): summed = lax.psum(weights.astype(jnp.float32), 'island')  52.7 us
    all_gather x1, waiting for transfers between devices, local(): lax.all_gather(weights, 'fsdp', axis=0, tiled=True)  35.5 us
    unnamed x18, local copies, waits for them, and re-layouts  22.2 us
    broadcast_in_dim x1, other arithmetic, local(): merged.astype(jnp.bfloat16)[None]  6.43 us
    dot_general x1, matrix products, local(): lax.dot_general(columns, key_grad, (((0,), (0,)), ((), ())), preferred_el...  3.25 us
    dot_general x1, matrix products, local(): jnp.dot(columns, lax.all_gather(weights, 'fsdp', axis=0, tiled=True), pre...  2.9 us
  transfers between devices with their start and end apart: 3, of which 2 were waited for; matrix products, arithmetic and copies ran while one was open for 14% of the time, Pallas kernels for 0%

commit v1 on v0

--- a/solution.py
+++ b/solution.py
@@ -1,3 +1,4 @@
+import functools
 import jax
 import jax.numpy as jnp
 from jax import lax
@@ -13,6 +14,14 @@
 outer_rate = 0.7
 outer_beta = 0.9
 merge_weight = 0.5
+
+
+def guide_sheet(matrix, group_axis):
+    heard = jnp.sum(lax.all_gather(matrix, group_axis), axis=0)
+    return heard
+
+
+spread_samples_all = functools.partial(guide_sheet, group_axis="island")
 
 
 def key_backward(keys, upstream):
@@ -34,7 +43,7 @@
     upstream = key_cotangent[0].astype(jnp.float32)
     scale = float(tokens.shape[1]) ** (-0.5)
     islands = lax.axis_size("island")
-    summed = lax.psum(weights.astype(jnp.float32), "island")
+    summed = spread_samples_all(weights.astype(jnp.float32))
     outer_grad = global_weights - summed / islands
     new_momentum = outer_beta * outer_momentum + outer_grad
     new_global = global_weights - outer_rate * (outer_grad + outer_beta * new_momentum)

time: 143 us -> 346 us (2.42)
  waiting for transfers between devices: 88.9 us -> 281 us
  other arithmetic: 8.62 us -> 16.5 us
  local copies, waits for them, and re-layouts: 22.8 us -> 27.7 us
    all_gather x0 -> x1, waiting for transfers between devices: none -> 212 us  [guide_sheet(): heard = jnp.sum(lax.all_gather(matrix, group_axis), axis=0)]
    psum x1 -> x0, waiting for transfers between devices: 52.7 us -> none  [local(): summed = lax.psum(weights.astype(jnp.float32), 'island')]
    reduce_scatter x1, waiting for transfers between devices: 0.01 us -> 32.6 us  [local(): lax.psum_scatter(lax.dot_general(columns, key_grad, (((0,), (0,)), ((), (...]
    reduce_sum x0 -> x1, other arithmetic: none -> 9.45 us  [guide_sheet(): heard = jnp.sum(lax.all_gather(matrix, group_axis), axis=0)]
  transfers between devices with their start and end apart: 3 -> 3, of which waited for: 2 -> 3; matrix products, arithmetic and copies ran while one was open for 14% -> 10% of each run, Pallas kernels for 0% -> 0%
where the time goes in v1:
time: 346 us; the launch traced here: 345 us
  waiting for transfers between devices  281 us (81%)
  local copies, waits for them, and re-layouts  27.7 us (8%)
  other arithmetic  16.5 us (5%)
  between operations  13.8 us (4%)
  matrix products  6.15 us (2%)
    all_gather x1, waiting for transfers between devices, guide_sheet(): heard = jnp.sum(lax.all_gather(matrix, group_axis), axis=0)  212 us
    all_gather x1, waiting for transfers between devices, local(): lax.all_gather(weights, 'fsdp', axis=0, tiled=True)  35.5 us
    reduce_scatter x1, waiting for transfers between devices, local(): lax.psum_scatter(lax.dot_general(columns, key_grad, (((0,), (0,)), ((), (...  32.6 us
    unnamed x18, local copies, waits for them, and re-layouts  22.4 us
    reduce_sum x1, other arithmetic, guide_sheet(): heard = jnp.sum(lax.all_gather(matrix, group_axis), axis=0)  9.45 us
  transfers between devices with their start and end apart: 3, of which 3 were waited for; matrix products, arithmetic and copies ran while one was open for 10% of the time, Pallas kernels for 0%

profile of v1, /device:TPU:0, one launch (start us, length us, event | category | flops | bytes accessed | tf_op | source)
XLA Modules:
  0.0 345.2 jit_solution(1921339373634203878)
XLA Ops:
  7.2 0.0 copy-start
  7.2 0.0 all-gather.6.cloned.1.call-start
  7.2 0.7 all-gather.6.cloned.1.call-update
  7.9 0.0 all-gather.4.cloned.1.call-start
  8.0 1.5 copy.35
  9.5 1.6 copy.38
  11.1 0.0 all-gather.4.cloned.1.call-update
  11.1 0.0 reduce-scatter.2.cloned.1.call-start
  11.2 0.1 reshape.52
  11.3 35.5 %all-gather.6.cloned.1.call-done = bf16[1,4096,512]{2,1,0:T(8,128)(2,1)} async-done(((bf16[1,1024,512]{2,1,0:T(8,128)(2,1)}), bf16[1,4096,512]{2,1,0:T(8,128)(2,1)}) %all-gather.6.cloned.1.call-update) | async-done | bytes 4194320 | tf_op jit(solution)/shard_map/all_gather | solution.py:54
  46.8 2.9 fusion.12
  49.7 0.1 reshape.50
  49.8 0.2 multiply_reduce_fusion.1
  50.0 0.4 multiply_reduce_fusion
  50.4 0.2 mul.112
  50.6 0.2 mul.107
  50.8 3.2 fusion
  54.1 0.0 reduce-scatter.2.cloned.1.call-update
  54.1 2.9 copy.41
  57.0 3.2 copy.42
  60.2 1.6 copy.36
  61.9 2.3 copy.37
  64.1 212.1 %all-gather.4.cloned.1.call-done = f32[8,1024,512]{2,1,0:T(8,128)} async-done(((f32[1,1024,512]{2,1,0:T(8,128)}), f32[8,1024,512]{2,1,0:T(8,128)}) %all-gather.4.cloned.1.call-update) | async-done | bytes 16777232 | tf_op jit(solution)/shard_map/all_gather | solution.py:20
  276.2 9.4 %reduce_sum.29 = f32[1024,512]{1,0:T(8,128)} reduce(f32[8,1024,512]{2,1,0:T(8,128)} %all-gather.4.cloned.1.call-done, f32[]{:T(128)} %constant.5.clone.1), dimensions={0}, to_apply=%region_3.0 | reduce | flops 3670016 | bytes 18874372 | tf_op jit(solution)/shard_map/reduce_sum | solution.py:20
  285.6 3.1 copy.39
  288.8 32.6 %reduce-scatter.2.cloned.1.call-done = bf16[1024,512]{0,1:T(8,128)(2,1)} async-done(((bf16[4096,512]{0,1:T(8,128)(2,1)}), bf16[1024,512]{0,1:T(8,128)(2,1)}) %reduce-scatter.2.cloned.1.call-update) | async-done | bytes 1048592 | tf_op jit(solution)/shard_map/reduce_scatter | solution.py:61
  321.4 6.4 %fusion.19 = (bf16[1,1024,512]{1,2,0:T(8,128)(2,1)}, f32[1024,512]{0,1:T(8,128)}, f32[1024,512]{0,1:T(8,128)}, bf16[1,1024,512]{1,2,0:T(8,128)(2,1)}, bf16[1,1024,512]{1,2,0:T(8,128)(2,1)}) fusion(bf16[1,1024,512]{1,2,0:T(8,128)(2,1)} %copy.37, bf16[1024,512]{0,1:T(8,128)(2,1)} %reduce-scatter.2.cloned.1.call-done, bf16[1,1024,512]{1,2,0:T(8,128)(2,1)S(1)} %copy.36, ...), kind=kLoop, calls=%fused_computation.25 | loop fusion | flops 15728640 | bytes 17825792 | tf_op jit(solution)/shard_map/broadcast_in_dim | solution.py:79
  327.8 2.9 copy.46
  330.7 2.9 copy.47
  333.6 2.4 copy.43
  336.0 1.3 copy.44
  337.3 1.3 copy.45
  (9 shorter events, 0.0 us)
Async XLA Ops:
  7.2 39.6 %copy-start = (bf16[1,128,4096]{2,1,0:T(8,128)(2,1)S(1)}, bf16[1,128,4096]{2,1,0:T(8,128)(2,1)}, u32[]{:S(2)}) copy-start(bf16[1,128,4096]{2,1,0:T(8,128)(2,1)} %param.12) | copy-start | bytes 3145732
  7.2 39.6 %all-gather.6.cloned.1.call-start = ((), (), s32[]{:S(2)}) async-start(), calls=%async_computation.3 | async-start | bytes 5242880 | tf_op jit(solution)/shard_map/all_gather | solution.py:54
  7.9 268.3 %all-gather.4.cloned.1.call-start = ((), (), s32[]{:S(2)}) async-start(), calls=%async_computation.2 | async-start | bytes 18874368 | tf_op jit(solution)/shard_map/all_gather | solution.py:20
  9.5 1.7 copy-start.3
  11.1 310.3 %reduce-scatter.2.cloned.1.call-start = ((), (), s32[]{:S(2)}) async-start(), calls=%async_computation.1 | async-start | bytes 5242880 | tf_op jit(solution)/shard_map/reduce_scatter | solution.py:61
  333.6 2.4 copy-start.2
  333.6 3.7 %copy-start.1 = (bf16[1,1024,512]{1,2,0:T(8,128)(2,1)S(1)}, bf16[1,1024,512]{1,2,0:T(8,128)(2,1)}, u32[]{:S(2)}) copy-start(bf16[1,1024,512]{1,2,0:T(8,128)(2,1)} %get-tuple-element.23) | copy-start | bytes 3145732
Sparse Core Ops, SparseCore 0:
  9.5 37.1 all-gather.5
  48.9 227.2 all-gather.3
  278.7 42.5 reduce-scatter.1
